TPU v7x, 128 devices: a whole 4x4x4 slice. The times are simulated.
128 devices in a mesh: seq: 16 (over x, z), hx: 8 (over y, core).
Axes of the slice: x: 4, y: 4, z: 4, core: 2. Of those that a mesh axis runs over, the one named last changes fastest.
Arguments:
- query: bfloat16 [16384, 8192], P('seq', 'hx'), may hold values from -6 to 6
- key_in: bfloat16 [16384, 8192], P('seq', 'hx'), may hold values from -6 to 6
- value: bfloat16 [16384, 8192], P('seq', 'hx'), may hold values from -6 to 6
- head_gain: float32 [8192], P('hx'), may hold values from 0.1 to 1.9
- out_weight: bfloat16 [8192, 6144], P('hx', 'seq'), may hold values from -0.0625 to 0.0625
- residual: bfloat16 [16384, 6144], P(('seq', 'hx')), may hold values from -6 to 6
Outputs:
- mixed: bfloat16 [16384, 6144], P(('seq', 'hx'))
All inputs are finite; a program needn't handle non-finite values.
Results may differ from a plain program's by a relative error of at most 0.014.
Values may be sent and summed in bfloat16 or wider, within the bound.
No kernel may reach another device: no remote copies, remote signals or barrier semaphores. Data moves between devices by JAX's collectives and lax.ppermute only.
A program may use at most 128 MiB of HBM per device.

v0:
```python
import jax
import jax.numpy as jnp
from jax import lax
from jax.sharding import PartitionSpec as P

DH = 128


def activate(array):
    return jax.nn.silu(array.astype(jnp.float32)).astype(jnp.bfloat16)


def per_device(query, key_in, value, head_gain, out_weight, residual):
    highest = lax.Precision.HIGHEST
    tokens_here, width = query.shape
    heads = width // DH
    q_act = activate(query).reshape(tokens_here, heads, DH)
    k_act = activate(key_in).reshape(tokens_here, heads, DH)
    v_heads = value.reshape(tokens_here, heads, DH)
    blocks = min(512, tokens_here)
    count = tokens_here // blocks
    rows = jnp.arange(blocks, dtype=jnp.int32)
    lower = rows[:, None] >= rows[None, :]
    running = jnp.zeros((heads, DH, DH), jnp.float32)
    pieces = []
    for index in range(count):
        q_part = q_act[index * blocks : (index + 1) * blocks]
        k_part = k_act[index * blocks : (index + 1) * blocks]
        v_part = v_heads[index * blocks : (index + 1) * blocks]
        scores = jnp.einsum("thd,shd->hts", q_part, k_part, preferred_element_type=jnp.float32)
        scores = jnp.where(lower[None, :, :], scores, jnp.zeros_like(scores))
        inner = jnp.einsum("hts,she->the", scores, v_part.astype(jnp.float32), precision=highest)
        if index > 0:
            inner = inner + jnp.einsum(
                "thd,hde->the", q_part.astype(jnp.float32), running, precision=highest
            )
        pieces.append(inner)
        running = running + jnp.einsum(
            "thd,the->hde", k_part, v_part, preferred_element_type=jnp.float32
        )
    local_part = jnp.concatenate(pieces, axis=0)
    empty = jnp.zeros((heads, DH, DH), jnp.float32)
    position = lax.axis_index("seq")
    piece = lax.all_gather(running[None].astype(jnp.bfloat16), "seq", axis=0, tiled=True).astype(
        jnp.float32
    )
    ranks = jnp.arange(piece.shape[0], dtype=jnp.int32)
    keep = (ranks < position)[:, None, None, None]
    prefix = empty + jnp.sum(jnp.where(keep, piece, jnp.zeros_like(piece)), axis=0)
    attended = local_part + jnp.einsum(
        "thd,hde->the", q_act.astype(jnp.float32), prefix, precision=highest
    )
    meansq = jnp.mean(attended * attended, axis=-1, keepdims=True)
    normed = attended * lax.rsqrt(meansq + 1e-06) * head_gain.reshape(heads, DH)
    normed = normed.astype(jnp.bfloat16).reshape(tokens_here, width)
    full_weight = lax.all_gather(out_weight, "seq", axis=1, tiled=True)
    summed = lax.psum_scatter(
        jnp.dot(normed, full_weight, preferred_element_type=jnp.float32).astype(jnp.bfloat16),
        "hx",
        scatter_dimension=0,
        tiled=True,
    ).astype(jnp.float32)
    return (summed + residual.astype(jnp.float32)).astype(jnp.bfloat16)


def solution(mesh):
    return jax.shard_map(
        per_device,
        mesh=mesh,
        in_specs=(
            P("seq", "hx"),
            P("seq", "hx"),
            P("seq", "hx"),
            P("hx"),
            P("hx", "seq"),
            P(("seq", "hx"), None),
        ),
        out_specs=P(("seq", "hx"), None),
        check_vma=False,
    )
```

profile of v0, /device:TPU:1, one launch (start us, length us, event | category | flops | bytes accessed | tf_op | source)
XLA Modules:
  0.0 277.5 jit_solution(6667149055458355304)
XLA Ops:
  6.5 2.9 %copy.46 = bf16[1024,1024]{0,1:T(8,128)(2,1)S(1)} copy(bf16[1024,1024]{1,0:T(8,128)(2,1)} %param.7) | data formatting | bytes 4194304 | tf_op args[1]
  9.4 1.2 fusion.12
  10.6 1.1 fusion.25
  11.8 1.3 fusion.24
  13.6 1.9 copy.78
  16.0 0.8 copy-done.7
  16.8 2.4 fusion.20
  19.2 0.7 all-gather.4.cloned.1.call-update
  20.0 4.0 %copy.45 = bf16[1024,1024]{0,1:T(8,128)(2,1)} copy(bf16[1024,1024]{1,0:T(8,128)(2,1)} %param.6) | data formatting | bytes 4194304 | tf_op args[0]
  24.1 2.9 %fusion.8 = bf16[1024,1024]{0,1:T(8,128)(2,1)S(1)} fusion(bf16[1024,1024]{0,1:T(8,128)(2,1)} %copy.45), kind=kLoop, calls=%fused_computation.14 | loop fusion | flops 6291456 | bytes 4194304 | tf_op jit(solution)/shard_map/convert_element_type | solution.py:10
  27.1 1.3 fusion.27
  28.4 4.5 %fusion.1 = f32[8,512,128]{2,1,0:T(8,128)S(1)} fusion(bf16[512,8,128]{0,2,1:T(8,128)(2,1)S(1)} %bitcast.41, f32[8,512,512]{2,1,0:T(8,128)S(1)} %fusion.27, pred[512,512]{1,0:T(8,128)(4,1)S(1)} %iota_compare_fusion), kind=kOutput, calls=%fused_computation.3 | convolution fusion | flops 3223322624 | bytes 11796480 | tf_op jit(solution)/shard_map/hts,she->the/dot_general | solution.py:32
  33.0 2.5 bitcast_add_fusion
  35.5 1.3 fusion.26
  36.8 6.0 %fusion.17 = f32[512,8,128]{2,0,1:T(8,128)} fusion(bf16[512,8,128]{0,2,1:T(8,128)(2,1)S(1)} %bitcast.37, f32[8,512,512]{2,1,0:T(8,128)S(1)} %fusion.26, pred[512,512]{1,0:T(8,128)(4,1)S(1)} %iota_compare_fusion), kind=kOutput, calls=%fused_computation.28 | convolution fusion | flops 3223322624 | bytes 11796480 | tf_op jit(solution)/shard_map/hts,she->the/dot_general | solution.py:32
  42.8 31.4 %all-gather.6.cloned.1.call-done = bf16[128,128,128]{2,1,0:T(8,128)(2,1)} async-done(((bf16[8,128,128]{2,1,0:T(8,128)(2,1)}), bf16[128,128,128]{2,1,0:T(8,128)(2,1)}) %all-gather.6.cloned.1.call-update) | async-done | bytes 4194320 | tf_op jit(solution)/shard_map/all_gather | solution.py:44
  74.2 3.3 %fusion = f32[8,128,128]{2,1,0:T(8,128)S(1)} fusion(bf16[16,8,128,128]{3,2,1,0:T(8,128)(2,1)} %bitcast.46, pred[16]{0:T(512)(128)(4,1)S(1)} %iota_compare_fusion.1), kind=kLoop, calls=%fused_computation.2 | loop fusion | flops 6160384 | bytes 4718608 | tf_op jit(solution)/shard_map/reduce_sum | solution.py:49
  77.7 3.3 %multiply_reduce_fusion = (f32[1024,8]{0,1:T(8,128)S(1)}, f32[1024,8,128]{2,0,1:T(8,128)S(1)}) fusion(f32[8,128,128]{2,1,0:T(8,128)S(1)} %fusion, bf16[1024,8,128]{0,2,1:T(8,128)(2,1)S(1)} %bitcast.35, f32[512,8,128]{2,0,1:T(8,128)S(1)} %copy-done.5, f32[512,8,128]{2,0,1:T(8,128)S(1)} %copy-done.6), kind=kOutput, calls=%fused_computation.21 | convolution fusion | flops 1614798848 | bytes 11042816 | tf_op jit(solution)/shard_map/thd,hde->the/dot_general | solution.py:50
  81.0 1.4 multiply_convert_fusion
  82.4 2.7 copy.63
  85.2 89.7 %all-gather.4.cloned.1.call-done = bf16[1024,6144]{1,0:T(8,128)(2,1)} async-done(((bf16[1024,384]{1,0:T(8,128)(2,1)}), bf16[1024,6144]{1,0:T(8,128)(2,1)}) %all-gather.4.cloned.1.call-update) | async-done | bytes 12582928 | tf_op jit(solution)/shard_map/all_gather | solution.py:56
  174.9 21.1 %convolution_convert_fusion = bf16[1024,6144]{1,0:T(8,128)(2,1)} fusion(bf16[1024,1024]{0,1:T(8,128)(2,1)} %bitcast.48, bf16[1024,6144]{1,0:T(8,128)(2,1)} %all-gather.4.cloned.1.call-done), kind=kOutput, calls=%fused_computation | convolution fusion | flops 12891193344 | bytes 27262976 | tf_op jit(solution)/shard_map/dot_general | solution.py:58
  195.9 72.1 %reduce-scatter.2.cloned.1.call-done = bf16[128,6144]{1,0:T(8,128)(2,1)} async-done(((bf16[1024,6144]{1,0:T(8,128)(2,1)}), bf16[128,6144]{1,0:T(8,128)(2,1)}) %reduce-scatter.2.cloned.1.call-update) | async-done | bytes 1572880 | tf_op jit(solution)/shard_map/reduce_scatter | solution.py:57
  268.0 2.9 %add_convert_fusion = bf16[128,6144]{1,0:T(8,128)(2,1)} fusion(bf16[128,6144]{1,0:T(8,128)(2,1)S(1)} %copy-done.10, bf16[128,6144]{1,0:T(8,128)(2,1)} %reduce-scatter.2.cloned.1.call-done), kind=kLoop, calls=%fused_computation.26 | loop fusion | flops 3145728 | bytes 4718592 | tf_op jit(solution)/shard_map/convert_element_type | solution.py:63
  (34 shorter events, 1.5 us)
Async XLA Ops:
  6.5 67.7 %all-gather.6.cloned.1.call-start = ((), (), s32[]{:S(2)}) async-start(), calls=%async_computation.3 | async-start | bytes 4456448 | tf_op jit(solution)/shard_map/all_gather | solution.py:44
  9.4 2.4 copy-start.9
  11.8 3.8 %copy-start = (bf16[512,1024]{0,1:T(8,128)(2,1)}, bf16[512,1024]{0,1:T(8,128)(2,1)S(1)}, u32[]{:S(2)}) copy-start(bf16[512,1024]{0,1:T(8,128)(2,1)S(1)} %get-tuple-element.9) | copy-start | bytes 3145732
  13.6 6.3 %copy-start.2 = (bf16[512,1024]{0,1:T(8,128)(2,1)}, bf16[512,1024]{0,1:T(8,128)(2,1)S(1)}, u32[]{:S(2)}) copy-start(bf16[512,1024]{0,1:T(8,128)(2,1)S(1)} %copy.79) | copy-start | bytes 3145732
  16.0 0.8 copy-start.7
  19.2 155.7 %all-gather.4.cloned.1.call-start = ((), (), s32[]{:S(2)}) async-start(), calls=%async_computation.1 | async-start | bytes 13369344 | tf_op jit(solution)/shard_map/all_gather | solution.py:56
  19.9 248.1 %reduce-scatter.2.cloned.1.call-start = ((), (), s32[]{:S(2)}) async-start(), calls=%async_computation.2 | async-start | bytes 14155776 | tf_op jit(solution)/shard_map/reduce_scatter | solution.py:57
  24.0 3.1 %copy-start.4 = (bf16[512,1024]{0,1:T(8,128)(2,1)S(1)}, bf16[512,1024]{0,1:T(8,128)(2,1)}, u32[]{:S(2)}) copy-start(bf16[512,1024]{0,1:T(8,128)(2,1)} %get-tuple-element.10) | copy-start | bytes 3145732
  27.1 1.3 copy-start.3
  28.4 4.6 %copy-start.8 = (f32[8,128,128]{2,1,0:T(8,128)S(1)}, f32[8,128,128]{2,1,0:T(8,128)}, u32[]{:S(2)}) copy-start(f32[8,128,128]{2,1,0:T(8,128)} %copy-done.7) | copy-start | bytes 1572868
  33.0 2.5 copy-start.1
  74.2 3.4 %copy-start.5 = (f32[512,8,128]{2,0,1:T(8,128)S(1)}, f32[512,8,128]{2,0,1:T(8,128)}, u32[]{:S(2)}) copy-start(f32[512,8,128]{2,0,1:T(8,128)} %bitcast_add_fusion) | copy-start | bytes 6291460
  74.2 3.5 %copy-start.6 = (f32[512,8,128]{2,0,1:T(8,128)S(1)}, f32[512,8,128]{2,0,1:T(8,128)}, u32[]{:S(2)}) copy-start(f32[512,8,128]{2,0,1:T(8,128)} %fusion.17) | copy-start | bytes 6291460
  77.7 3.3 %copy-start.11 = (f32[1024]{0:T(1024)S(1)}, f32[1024]{0:T(1024)}, u32[]{:S(2)}) copy-start(f32[1024]{0:T(1024)} %param.9) | copy-start | bytes 12292
  195.9 72.1 %copy-start.10 = (bf16[128,6144]{1,0:T(8,128)(2,1)S(1)}, bf16[128,6144]{1,0:T(8,128)(2,1)}, u32[]{:S(2)}) copy-start(bf16[128,6144]{1,0:T(8,128)(2,1)} %param.11) | copy-start | bytes 4718596
Sparse Core Ops, SparseCore 0:
  19.3 54.8 all-gather.5
  76.3 98.4 all-gather.3
  196.1 71.9 reduce-scatter.1
where the time goes:
time: 278 us; the launch traced here: 277 us
  waiting for transfers between devices  194 us (70%)
  matrix products  42.7 us (15%)
  local copies, waits for them, and re-layouts  15.5 us (6%)
  between operations  13.3 us (5%)
  other arithmetic  11.9 us (4%)
    all_gather x1, waiting for transfers between devices, per_device(): full_weight = lax.all_gather(out_weight, 'seq', axis=1, tiled=True)  89.7 us
    reduce_scatter x1, waiting for transfers between devices, per_device(): lax.psum_scatter(jnp.dot(normed, full_weight, preferred_element_type=jnp....  72.1 us
    all_gather x1, waiting for transfers between devices, per_device(): lax.all_gather(running[None].astype(jnp.bfloat16), 'seq', axis=0, tiled=T...  31.4 us
    dot_general x1, matrix products, per_device(): jnp.dot(normed, full_weight, preferred_element_type=jnp.float32)  21.1 us
    dot_general x2, matrix products, per_device(): jnp.einsum('hts,she->the', scores, v_part.astype(jnp.float32), precision=...  10.5 us
    unnamed x28, local copies, waits for them, and re-layouts  10.2 us
  transfers between devices with their start and end apart: 3, of which 3 were waited for; matrix products, arithmetic and copies ran while one was open for 12% of the time, Pallas kernels for 0%

commit v1 on v0

--- a/solution.py
+++ b/solution.py
@@ -4,6 +4,25 @@
 from jax.sharding import PartitionSpec as P
 
 DH = 128
+
+
+def _wrap_task(payload):
+    full_n = lax.axis_size("seq")
+    w1 = map(lambda j0: (j0, (j0 + 1) % full_n), range(full_n))
+    log = list(w1)
+    small = range(full_n)
+    near = map(lambda j0: (j0, (j0 - 1) % full_n), small)
+    inbox = list(near)
+    low, current_value = ([payload], [payload])
+    for _ in range(full_n // 2):
+        low.append(lax.ppermute(low[-1], perm=log, axis_name="seq"))
+    rr = 0
+    while rr < (full_n - 1) // 2:
+        current_value.append(lax.ppermute(current_value[-1], axis_name="seq", perm=inbox))
+        rr = rr + 1
+    a_next = jnp.concatenate([*low[::-1], *current_value[1:]], axis=1)
+    prior = lax.axis_index("seq")
+    return jnp.roll(a_next, (prior - full_n // 2) * payload.shape[1], axis=1)
 
 
 def activate(array):
@@ -53,7 +72,7 @@
     meansq = jnp.mean(attended * attended, axis=-1, keepdims=True)
     normed = attended * lax.rsqrt(meansq + 1e-06) * head_gain.reshape(heads, DH)
     normed = normed.astype(jnp.bfloat16).reshape(tokens_here, width)
-    full_weight = lax.all_gather(out_weight, "seq", axis=1, tiled=True)
+    full_weight = _wrap_task(out_weight)
     summed = lax.psum_scatter(
         jnp.dot(normed, full_weight, preferred_element_type=jnp.float32).astype(jnp.bfloat16),
         "hx",

time: 278 us -> 362 us (1.30)
  local copies, waits for them, and re-layouts: 15.5 us -> 74.7 us
  starting transfers between devices: 0.08 us -> 37.6 us
  waiting for transfers between devices: 194 us -> 169 us
  matrix products: 42.7 us -> 52.2 us
    ppermute x0 -> x15, waiting for transfers between devices: none -> 98.2 us  [the longest x8 68.2 us: _wrap_task(): low.append(lax.ppermute(low[-1], perm=log, axis_name='seq'))]
    all_gather x1 -> x0, waiting for transfers between devices: 89.7 us -> none  [per_device(): full_weight = lax.all_gather(out_weight, 'seq', axis=1, tiled=True)]
    unnamed x28 -> x69, local copies, waits for them, and re-layouts: 10.2 us -> 67.5 us
    ppermute x0 -> x15, starting transfers between devices: none -> 37.6 us  [the longest x7 35.1 us: _wrap_task(): lax.ppermute(current_value[-1], axis_name='seq', perm=inbox)]
    all_gather x1, waiting for transfers between devices: 31.4 us -> 0.01 us  [per_device(): lax.all_gather(running[None].astype(jnp.bfloat16), 'seq', axis=0, tiled=T...]
    dot_general x2, matrix products: 2.58 us -> 8.61 us  [per_device(): jnp.einsum('thd,shd->hts', q_part, k_part, preferred_element_type=jnp.flo...]
  transfers between devices with their start and end apart: 3 -> 17, of which waited for: 3 -> 11; matrix products, arithmetic and copies ran while one was open for 12% -> 29% of each run, Pallas kernels for 0% -> 0%
where the time goes in v1:
time: 362 us; the launch traced here: 361 us
  waiting for transfers between devices  169 us (47%)
  local copies, waits for them, and re-layouts  74.7 us (21%)
  matrix products  52.2 us (14%)
  starting transfers between devices  37.6 us (10%)
  between operations  13.7 us (4%)
  other arithmetic  13.1 us (4%)
    reduce_scatter x1, waiting for transfers between devices, per_device(): lax.psum_scatter(jnp.dot(normed, full_weight, preferred_element_type=jnp....  71.1 us
    ppermute x8, waiting for transfers between devices, _wrap_task(): low.append(lax.ppermute(low[-1], perm=log, axis_name='seq'))  68.2 us
    unnamed x69, local copies, waits for them, and re-layouts  67.5 us
    ppermute x7, starting transfers between devices, _wrap_task(): lax.ppermute(current_value[-1], axis_name='seq', perm=inbox)  35.1 us
    ppermute x7, waiting for transfers between devices, _wrap_task(): lax.ppermute(current_value[-1], axis_name='seq', perm=inbox)  29.9 us
    dot_general x1, matrix products, per_device(): jnp.dot(normed, full_weight, preferred_element_type=jnp.float32)  21.9 us
    dot_general x2, matrix products, per_device(): jnp.einsum('hts,she->the', scores, v_part.astype(jnp.float32), precision=...  12.8 us
    dot_general x2, matrix products, per_device(): jnp.einsum('thd,shd->hts', q_part, k_part, preferred_element_type=jnp.flo...  8.61 us
  transfers between devices with their start and end apart: 17, of which 11 were waited for; matrix products, arithmetic and copies ran while one was open for 29% of the time, Pallas kernels for 0%

profile of v1, /device:TPU:1, one launch (start us, length us, event | category | flops | bytes accessed | tf_op | source)
XLA Modules:
  0.0 360.6 jit_solution(535126083509305440)
XLA Ops:
  9.0 21.8 %collective-permute-done = bf16[1024,384]{1,0:T(8,128)(2,1)S(1)} collective-permute-done((bf16[1024,384]{1,0:T(8,128)(2,1)}, bf16[1024,384]{1,0:T(8,128)(2,1)S(1)}, u32[]{:S(2)}, u32[]{:S(2)}) %collective-permute-start) | collective-permute-done | bytes 786464 | tf_op jit(solution)/shard_map/ppermute | solution.py:18
  30.8 4.8 %collective-permute-start.8 = (bf16[1024,384]{1,0:T(8,128)(2,1)}, bf16[1024,384]{1,0:T(8,128)(2,1)}, u32[]{:S(2)}, u32[]{:S(2)}) collective-permute-start(bf16[1024,384]{1,0:T(8,128)(2,1)} %param.10), channel_id=1, source_target_pairs={{0,120},{8,0},{16,8},{24,16},{32,24},{40,32},{48,40},{56,48},{64,5... | collective-permute-start | bytes 2359304 | tf_op jit(solution)/shard_map/ppermute | solution.py:21
  35.6 16.3 %collective-permute-done.1 = bf16[1024,384]{1,0:T(8,128)(2,1)S(1)} collective-permute-done((bf16[1024,384]{1,0:T(8,128)(2,1)S(1)}, bf16[1024,384]{1,0:T(8,128)(2,1)S(1)}, u32[]{:S(2)}, u32[]{:S(2)}) %collective-permute-start.1) | collective-permute-done | bytes 786464 | tf_op jit(solution)/shard_map/ppermute | solution.py:18
  51.9 3.1 copy.46
  57.7 4.5 %collective-permute-start.9 = (bf16[1024,384]{1,0:T(8,128)(2,1)}, bf16[1024,384]{1,0:T(8,128)(2,1)}, u32[]{:S(2)}, u32[]{:S(2)}) collective-permute-start(bf16[1024,384]{1,0:T(8,128)(2,1)} %collective-permute-done.8), channel_id=1, source_target_pairs={{0,120},{8,0},{16,8},{24,16},{32,24},{40,32},{48,40},{56,48},{64,5... | collective-permute-start | bytes 2359304 | tf_op jit(solution)/shard_map/ppermute | solution.py:21
  62.2 10.1 %collective-permute-done.2 = bf16[1024,384]{1,0:T(8,128)(2,1)} collective-permute-done((bf16[1024,384]{1,0:T(8,128)(2,1)S(1)}, bf16[1024,384]{1,0:T(8,128)(2,1)}, u32[]{:S(2)}, u32[]{:S(2)}) %collective-permute-start.2) | collective-permute-done | bytes 786464 | tf_op jit(solution)/shard_map/ppermute | solution.py:18
  77.2 5.2 %collective-permute-start.10 = (bf16[1024,384]{1,0:T(8,128)(2,1)}, bf16[1024,384]{1,0:T(8,128)(2,1)}, u32[]{:S(2)}, u32[]{:S(2)}) collective-permute-start(bf16[1024,384]{1,0:T(8,128)(2,1)} %collective-permute-done.9), channel_id=1, source_target_pairs={{0,120},{8,0},{16,8},{24,16},{32,24},{40,32},{48,40},{56,48},{64,5... | collective-permute-start | bytes 2359304 | tf_op jit(solution)/shard_map/ppermute | solution.py:21
  82.4 9.4 %collective-permute-done.3 = bf16[1024,384]{1,0:T(8,128)(2,1)} collective-permute-done((bf16[1024,384]{1,0:T(8,128)(2,1)}, bf16[1024,384]{1,0:T(8,128)(2,1)}, u32[]{:S(2)}, u32[]{:S(2)}) %collective-permute-start.3) | collective-permute-done | bytes 786464 | tf_op jit(solution)/shard_map/ppermute | solution.py:18
  93.1 3.9 %copy.45 = bf16[1024,1024]{0,1:T(8,128)(2,1)} copy(bf16[1024,1024]{1,0:T(8,128)(2,1)} %param.6) | data formatting | bytes 4194304 | tf_op args[0]
  97.0 2.9 fusion.13
  100.0 4.8 %collective-permute-start.11 = (bf16[1024,384]{1,0:T(8,128)(2,1)}, bf16[1024,384]{1,0:T(8,128)(2,1)S(1)}, u32[]{:S(2)}, u32[]{:S(2)}) collective-permute-start(bf16[1024,384]{1,0:T(8,128)(2,1)} %collective-permute-done.10), channel_id=1, source_target_pairs={{0,120},{8,0},{16,8},{24,16},{32,24},{40,32},{48,40},{56,48},{64,5... | collective-permute-start | bytes 2359304 | tf_op jit(solution)/shard_map/ppermute | solution.py:21
  104.8 5.7 %collective-permute-done.4 = bf16[1024,384]{1,0:T(8,128)(2,1)} collective-permute-done((bf16[1024,384]{1,0:T(8,128)(2,1)}, bf16[1024,384]{1,0:T(8,128)(2,1)}, u32[]{:S(2)}, u32[]{:S(2)}) %collective-permute-start.4) | collective-permute-done | bytes 786464 | tf_op jit(solution)/shard_map/ppermute | solution.py:18
  113.2 10.0 %collective-permute-done.11 = bf16[1024,384]{1,0:T(8,128)(2,1)S(1)} collective-permute-done((bf16[1024,384]{1,0:T(8,128)(2,1)}, bf16[1024,384]{1,0:T(8,128)(2,1)S(1)}, u32[]{:S(2)}, u32[]{:S(2)}) %collective-permute-start.11) | collective-permute-done | bytes 786464 | tf_op jit(solution)/shard_map/ppermute | solution.py:21
  123.2 5.4 %collective-permute-start.12 = (bf16[1024,384]{1,0:T(8,128)(2,1)S(1)}, bf16[1024,384]{1,0:T(8,128)(2,1)}, u32[]{:S(2)}, u32[]{:S(2)}) collective-permute-start(bf16[1024,384]{1,0:T(8,128)(2,1)S(1)} %collective-permute-done.11), channel_id=1, source_target_pairs={{0,120},{8,0},{16,8},{24,16},{32,24},{40,32},{48,40},{56,48},{64,5... | collective-permute-start | bytes 2359304 | tf_op jit(solution)/shard_map/ppermute | solution.py:21
  131.5 6.1 %fusion.32 = f32[8,512,512]{2,1,0:T(8,128)} fusion(bf16[512,8,128]{0,2,1:T(8,128)(2,1)S(1)} %bitcast.46, bf16[512,8,128]{0,2,1:T(8,128)(2,1)} %bitcast.40), kind=kOutput, calls=%fused_computation.74 | convolution fusion | flops 536870912 | bytes 10485760 | tf_op jit(solution)/shard_map/thd,shd->hts/dot_general | solution.py:49
  137.6 4.5 %fusion.6 = f32[8,512,128]{2,1,0:T(8,128)S(1)} fusion(bf16[512,8,128]{0,2,1:T(8,128)(2,1)S(1)} %bitcast.38, f32[8,512,512]{2,1,0:T(8,128)S(1)} %fusion.33, pred[512,512]{1,0:T(8,128)(4,1)S(1)} %iota_compare_fusion), kind=kOutput, calls=%fused_computation.5 | convolution fusion | flops 3223322624 | bytes 11796480 | tf_op jit(solution)/shard_map/hts,she->the/dot_general | solution.py:51
  142.2 4.8 %collective-permute-start.13 = (bf16[1024,384]{1,0:T(8,128)(2,1)}, bf16[1024,384]{1,0:T(8,128)(2,1)}, u32[]{:S(2)}, u32[]{:S(2)}) collective-permute-start(bf16[1024,384]{1,0:T(8,128)(2,1)} %collective-permute-done.12), channel_id=1, source_target_pairs={{0,120},{8,0},{16,8},{24,16},{32,24},{40,32},{48,40},{56,48},{64,5... | collective-permute-start | bytes 2359304 | tf_op jit(solution)/shard_map/ppermute | solution.py:21
  151.1 8.2 %fusion.22 = f32[512,8,128]{2,0,1:T(8,128)} fusion(bf16[512,8,128]{0,2,1:T(8,128)(2,1)S(1)} %bitcast.36, f32[8,512,512]{2,1,0:T(8,128)} %fusion.32, pred[512,512]{1,0:T(8,128)(4,1)S(1)} %iota_compare_fusion), kind=kOutput, calls=%fused_computation.30 | convolution fusion | flops 3223322624 | bytes 11796480 | tf_op jit(solution)/shard_map/hts,she->the/dot_general | solution.py:51
  159.3 19.9 %collective-permute-done.13 = bf16[1024,384]{1,0:T(8,128)(2,1)} collective-permute-done((bf16[1024,384]{1,0:T(8,128)(2,1)}, bf16[1024,384]{1,0:T(8,128)(2,1)}, u32[]{:S(2)}, u32[]{:S(2)}) %collective-permute-start.13) | collective-permute-done | bytes 786464 | tf_op jit(solution)/shard_map/ppermute | solution.py:21
  179.2 5.5 %collective-permute-start.14 = (bf16[1024,384]{1,0:T(8,128)(2,1)}, bf16[1024,384]{1,0:T(8,128)(2,1)S(1)}, u32[]{:S(2)}, u32[]{:S(2)}) collective-permute-start(bf16[1024,384]{1,0:T(8,128)(2,1)} %collective-permute-done.13), channel_id=1, source_target_pairs={{0,120},{8,0},{16,8},{24,16},{32,24},{40,32},{48,40},{56,48},{64,5... | collective-permute-start | bytes 2359304 | tf_op jit(solution)/shard_map/ppermute | solution.py:21
  245.7 3.2 fusion.5
  248.9 4.8 %multiply_reduce_fusion = (f32[1024,8]{0,1:T(8,128)S(1)}, f32[1024,8,128]{2,0,1:T(8,128)S(1)}) fusion(f32[8,128,128]{2,1,0:T(8,128)S(1)} %fusion.5, bf16[1024,8,128]{0,2,1:T(8,128)(2,1)S(1)} %bitcast.34, f32[512,8,128]{2,0,1:T(8,128)} %bitcast_add_fusion, f32[512,8,128]{2,0,1:T(8,128)} %fusion.22), kind=kOutput, calls=%fused_computation.23 | convolution fusion | flops 1614798848 | bytes 11042816 | tf_op jit(solution)/shard_map/thd,hde->the/dot_general | solution.py:69
  257.9 21.9 %fusion.2 = bf16[1024,6144]{1,0:T(8,128)(2,1)} fusion(bf16[1024,1024]{0,1:T(8,128)(2,1)} %bitcast.47, bf16[1024,12288]{1,0:T(8,128)(2,1)} %constant_dynamic-update-slice_fusion, s32[]{:T(128)S(6)} %select_n.28), kind=kOutput, calls=%fused_computation.2 | convolution fusion | flops 12891193344 | bytes 27262980 | tf_op jit(solution)/shard_map/dot_general | solution.py:77
  279.8 71.1 %reduce-scatter.2.cloned.1.call-done = bf16[128,6144]{1,0:T(8,128)(2,1)} async-done(((bf16[1024,6144]{1,0:T(8,128)(2,1)}), bf16[128,6144]{1,0:T(8,128)(2,1)}) %reduce-scatter.2.cloned.1.call-update) | async-done | bytes 1572880 | tf_op jit(solution)/shard_map/reduce_scatter | solution.py:76
  (103 shorter events, 88.7 us)
Async XLA Ops:
  6.5 239.2 %all-gather.3.cloned.1.call-start = ((), (), s32[]{:S(2)}) async-start(), calls=%async_computation.2 | async-start | bytes 4456448 | tf_op jit(solution)/shard_map/all_gather | solution.py:63
  6.5 24.3 %collective-permute-start = (bf16[1024,384]{1,0:T(8,128)(2,1)}, bf16[1024,384]{1,0:T(8,128)(2,1)S(1)}, u32[]{:S(2)}, u32[]{:S(2)}) collective-permute-start(bf16[1024,384]{1,0:T(8,128)(2,1)} %param.10), channel_id=1, source_target_pairs={{0,8},{8,16},{16,24},{24,32},{32,40},{40,48},{48,56},{56,64},{64,7... | collective-permute-start | bytes 2359304 | tf_op jit(solution)/shard_map/ppermute | solution.py:18
  30.8 21.1 %collective-permute-start.1 = (bf16[1024,384]{1,0:T(8,128)(2,1)S(1)}, bf16[1024,384]{1,0:T(8,128)(2,1)S(1)}, u32[]{:S(2)}, u32[]{:S(2)}) collective-permute-start(bf16[1024,384]{1,0:T(8,128)(2,1)S(1)} %collective-permute-done), channel_id=1, source_target_pairs={{0,8},{8,16},{16,24},{24,32},{32,40},{40,48},{48,56},{56,64},{64,7... | collective-permute-start | bytes 2359304 | tf_op jit(solution)/shard_map/ppermute | solution.py:18
  30.8 26.9 %collective-permute-start.8 = (bf16[1024,384]{1,0:T(8,128)(2,1)}, bf16[1024,384]{1,0:T(8,128)(2,1)}, u32[]{:S(2)}, u32[]{:S(2)}) collective-permute-start(bf16[1024,384]{1,0:T(8,128)(2,1)} %param.10), channel_id=1, source_target_pairs={{0,120},{8,0},{16,8},{24,16},{32,24},{40,32},{48,40},{56,48},{64,5... | collective-permute-start | bytes 2359304 | tf_op jit(solution)/shard_map/ppermute | solution.py:21
  51.9 20.3 %collective-permute-start.2 = (bf16[1024,384]{1,0:T(8,128)(2,1)S(1)}, bf16[1024,384]{1,0:T(8,128)(2,1)}, u32[]{:S(2)}, u32[]{:S(2)}) collective-permute-start(bf16[1024,384]{1,0:T(8,128)(2,1)S(1)} %collective-permute-done.1), channel_id=1, source_target_pairs={{0,8},{8,16},{16,24},{24,32},{32,40},{40,48},{48,56},{56,64},{64,7... | collective-permute-start | bytes 2359304 | tf_op jit(solution)/shard_map/ppermute | solution.py:18
  57.7 19.6 %collective-permute-start.9 = (bf16[1024,384]{1,0:T(8,128)(2,1)}, bf16[1024,384]{1,0:T(8,128)(2,1)}, u32[]{:S(2)}, u32[]{:S(2)}) collective-permute-start(bf16[1024,384]{1,0:T(8,128)(2,1)} %collective-permute-done.8), channel_id=1, source_target_pairs={{0,120},{8,0},{16,8},{24,16},{32,24},{40,32},{48,40},{56,48},{64,5... | collective-permute-start | bytes 2359304 | tf_op jit(solution)/shard_map/ppermute | solution.py:21
  72.2 19.6 %collective-permute-start.3 = (bf16[1024,384]{1,0:T(8,128)(2,1)}, bf16[1024,384]{1,0:T(8,128)(2,1)}, u32[]{:S(2)}, u32[]{:S(2)}) collective-permute-start(bf16[1024,384]{1,0:T(8,128)(2,1)} %collective-permute-done.2), channel_id=1, source_target_pairs={{0,8},{8,16},{16,24},{24,32},{32,40},{40,48},{48,56},{56,64},{64,7... | collective-permute-start | bytes 2359304 | tf_op jit(solution)/shard_map/ppermute | solution.py:18
  77.2 22.7 %collective-permute-start.10 = (bf16[1024,384]{1,0:T(8,128)(2,1)}, bf16[1024,384]{1,0:T(8,128)(2,1)}, u32[]{:S(2)}, u32[]{:S(2)}) collective-permute-start(bf16[1024,384]{1,0:T(8,128)(2,1)} %collective-permute-done.9), channel_id=1, source_target_pairs={{0,120},{8,0},{16,8},{24,16},{32,24},{40,32},{48,40},{56,48},{64,5... | collective-permute-start | bytes 2359304 | tf_op jit(solution)/shard_map/ppermute | solution.py:21
  91.8 18.7 %collective-permute-start.4 = (bf16[1024,384]{1,0:T(8,128)(2,1)}, bf16[1024,384]{1,0:T(8,128)(2,1)}, u32[]{:S(2)}, u32[]{:S(2)}) collective-permute-start(bf16[1024,384]{1,0:T(8,128)(2,1)} %collective-permute-done.3), channel_id=1, source_target_pairs={{0,8},{8,16},{16,24},{24,32},{32,40},{40,48},{48,56},{56,64},{64,7... | collective-permute-start | bytes 2359304 | tf_op jit(solution)/shard_map/ppermute | solution.py:18
  93.0 257.8 %reduce-scatter.2.cloned.1.call-start = ((), (), s32[]{:S(2)}) async-start(), calls=%async_computation.1 | async-start | bytes 14155776 | tf_op jit(solution)/shard_map/reduce_scatter | solution.py:76
  97.0 51.5 %copy-start.5 = (f32[8,128,128]{2,1,0:T(8,128)S(1)}, f32[8,128,128]{2,1,0:T(8,128)}, u32[]{:S(2)}) copy-start(f32[8,128,128]{2,1,0:T(8,128)} %copy-done.4) | copy-start | bytes 1572868
  100.0 23.2 %collective-permute-start.11 = (bf16[1024,384]{1,0:T(8,128)(2,1)}, bf16[1024,384]{1,0:T(8,128)(2,1)S(1)}, u32[]{:S(2)}, u32[]{:S(2)}) collective-permute-start(bf16[1024,384]{1,0:T(8,128)(2,1)} %collective-permute-done.10), channel_id=1, source_target_pairs={{0,120},{8,0},{16,8},{24,16},{32,24},{40,32},{48,40},{56,48},{64,5... | collective-permute-start | bytes 2359304 | tf_op jit(solution)/shard_map/ppermute | solution.py:21
  110.5 20.9 %collective-permute-start.5 = (bf16[1024,384]{1,0:T(8,128)(2,1)}, bf16[1024,384]{1,0:T(8,128)(2,1)S(1)}, u32[]{:S(2)}, u32[]{:S(2)}) collective-permute-start(bf16[1024,384]{1,0:T(8,128)(2,1)} %collective-permute-done.4), channel_id=1, source_target_pairs={{0,8},{8,16},{16,24},{24,32},{32,40},{40,48},{48,56},{56,64},{64,7... | collective-permute-start | bytes 2359304 | tf_op jit(solution)/shard_map/ppermute | solution.py:18
  123.2 19.0 %collective-permute-start.12 = (bf16[1024,384]{1,0:T(8,128)(2,1)S(1)}, bf16[1024,384]{1,0:T(8,128)(2,1)}, u32[]{:S(2)}, u32[]{:S(2)}) collective-permute-start(bf16[1024,384]{1,0:T(8,128)(2,1)S(1)} %collective-permute-done.11), channel_id=1, source_target_pairs={{0,120},{8,0},{16,8},{24,16},{32,24},{40,32},{48,40},{56,48},{64,5... | collective-permute-start | bytes 2359304 | tf_op jit(solution)/shard_map/ppermute | solution.py:21
  131.5 17.0 %collective-permute-start.6 = (bf16[1024,384]{1,0:T(8,128)(2,1)S(1)}, bf16[1024,384]{1,0:T(8,128)(2,1)}, u32[]{:S(2)}, u32[]{:S(2)}) collective-permute-start(bf16[1024,384]{1,0:T(8,128)(2,1)S(1)} %collective-permute-done.5), channel_id=1, source_target_pairs={{0,8},{8,16},{16,24},{24,32},{32,40},{40,48},{48,56},{56,64},{64,7... | collective-permute-start | bytes 2359304 | tf_op jit(solution)/shard_map/ppermute | solution.py:18
  142.2 37.0 %collective-permute-start.13 = (bf16[1024,384]{1,0:T(8,128)(2,1)}, bf16[1024,384]{1,0:T(8,128)(2,1)}, u32[]{:S(2)}, u32[]{:S(2)}) collective-permute-start(bf16[1024,384]{1,0:T(8,128)(2,1)} %collective-permute-done.12), channel_id=1, source_target_pairs={{0,120},{8,0},{16,8},{24,16},{32,24},{40,32},{48,40},{56,48},{64,5... | collective-permute-start | bytes 2359304 | tf_op jit(solution)/shard_map/ppermute | solution.py:21
  148.5 36.8 %collective-permute-start.7 = (bf16[1024,384]{1,0:T(8,128)(2,1)}, bf16[1024,384]{1,0:T(8,128)(2,1)}, u32[]{:S(2)}, u32[]{:S(2)}) collective-permute-start(bf16[1024,384]{1,0:T(8,128)(2,1)} %collective-permute-done.6), channel_id=1, source_target_pairs={{0,8},{8,16},{16,24},{24,32},{32,40},{40,48},{48,56},{56,64},{64,7... | collective-permute-start | bytes 2359304 | tf_op jit(solution)/shard_map/ppermute | solution.py:18
  151.0 60.3 %copy-start.12 = (bf16[1024,384]{1,0:T(8,128)(2,1)S(1)}, bf16[1024,384]{1,0:T(8,128)(2,1)}, u32[]{:S(2)}) copy-start(bf16[1024,384]{1,0:T(8,128)(2,1)} %copy-done.11) | copy-start | bytes 2359300
  151.0 71.0 %copy-start.14 = (bf16[1024,384]{1,0:T(8,128)(2,1)S(1)}, bf16[1024,384]{1,0:T(8,128)(2,1)}, u32[]{:S(2)}) copy-start(bf16[1024,384]{1,0:T(8,128)(2,1)} %copy-done.13) | copy-start | bytes 2359300
  151.0 78.5 %copy-start.10 = (bf16[1024,384]{1,0:T(8,128)(2,1)S(1)}, bf16[1024,384]{1,0:T(8,128)(2,1)}, u32[]{:S(2)}) copy-start(bf16[1024,384]{1,0:T(8,128)(2,1)} %copy-done.9) | copy-start | bytes 2359300
  151.0 79.5 %copy-start.8 = (bf16[1024,384]{1,0:T(8,128)(2,1)S(1)}, bf16[1024,384]{1,0:T(8,128)(2,1)}, u32[]{:S(2)}) copy-start(bf16[1024,384]{1,0:T(8,128)(2,1)} %copy-done.7) | copy-start | bytes 2359300
  151.0 80.5 %copy-start.6 = (bf16[1024,384]{1,0:T(8,128)(2,1)S(1)}, bf16[1024,384]{1,0:T(8,128)(2,1)}, u32[]{:S(2)}) copy-start(bf16[1024,384]{1,0:T(8,128)(2,1)} %param.10) | copy-start | bytes 2359300
  179.2 37.5 %collective-permute-start.14 = (bf16[1024,384]{1,0:T(8,128)(2,1)}, bf16[1024,384]{1,0:T(8,128)(2,1)S(1)}, u32[]{:S(2)}, u32[]{:S(2)}) collective-permute-start(bf16[1024,384]{1,0:T(8,128)(2,1)} %collective-permute-done.13), channel_id=1, source_target_pairs={{0,120},{8,0},{16,8},{24,16},{32,24},{40,32},{48,40},{56,48},{64,5... | collective-permute-start | bytes 2359304 | tf_op jit(solution)/shard_map/ppermute | solution.py:21
  257.9 93.0 %copy-start.15 = (bf16[128,6144]{1,0:T(8,128)(2,1)S(1)}, bf16[128,6144]{1,0:T(8,128)(2,1)}, u32[]{:S(2)}) copy-start(bf16[128,6144]{1,0:T(8,128)(2,1)} %param.11) | copy-start | bytes 4718596
  (10 other events, 240.9 us)
Sparse Core Ops, SparseCore 0:
  93.2 92.1 all-gather.2
  279.9 70.9 reduce-scatter.1
